TPU v7x, 32 devices: a whole 2x2x4 slice. The times are simulated.
32 devices in a mesh: grp: 2 (over x), seq: 16 (over z, y, core).
Axes of the slice: x: 2, y: 2, z: 4, core: 2. Of those that a mesh axis runs over, the one named last changes fastest.
Arguments:
- queries: bfloat16 [8192, 8192], P(('grp', 'seq')), parts along dimension 0, may hold values from -6 to 6
- keys_in: bfloat16 [8192, 8192], P(('grp', 'seq')), parts along dimension 0, may hold values from -0.375 to 0.375
- values_in: bfloat16 [8192, 8192], P(('grp', 'seq')), parts along dimension 0, may hold values from -6 to 6
- log_decay: bfloat16 [8192, 64], P(('grp', 'seq')), parts along dimension 0, may hold values from -2 to 0, as said below
- gate_logits: bfloat16 [8192, 8192], P(('grp', 'seq')), parts along dimension 0, may hold values from -6 to 6
- norm_gain: float32 [8192], replicated, may hold values from 0.1 to 1.9
- doc_lengths: int32 [16], P('grp'), parts along dimension 0, may hold values from 1 to 2048, 4096 in all
Outputs:
- attended: bfloat16 [8192, 8192], P(('grp', 'seq')), parts along dimension 0
- final_state: float32 [128, 128, 128], P(('grp', 'seq')), parts along dimension 0
There are 2 independent parts, one for each index of `grp`. A program takes and returns all parts, laid end to end along the dimension named above; an argument that names none is the same for every part. Nothing has to cross between parts.
Inputs may be any that keep to these rules, and one draw needn't show every extreme that they name: log_decay is negative. `doc_lengths`: the 8 lengths are positive and sum to 4096.
All inputs are finite; a program needn't handle non-finite values.
Results may differ from a plain program's by a relative error of at most 0.0049.
Values may be sent and summed in bfloat16 or wider, within the bound.
A program may use at most 320 MiB of HBM per device.

v0:
```python
import math

import jax
import jax.numpy as jnp
from jax import lax
from jax.sharding import PartitionSpec as P

HEADS = 64
HEAD_DIM = 128
SPAN = 256


EPS = 1e-05


def doc_index(doc_lengths, positions):
    doc_ends = jnp.cumsum(doc_lengths)
    return jnp.sum((positions[:, None] >= doc_ends[None, :]).astype(jnp.int32), axis=1)


def local_terms(query_blk, key_blk, value_blk, decay_blk, doc_blk, prior_doc):
    length = query_blk.shape[1]
    row_index = lax.broadcasted_iota(jnp.int32, (length, length), 0)
    col_index = lax.broadcasted_iota(jnp.int32, (length, length), 1)
    causal = row_index >= col_index
    cumulative = jnp.einsum(
        "ij,gjh->gih", causal.astype(jnp.float32), decay_blk, precision=lax.Precision.HIGHEST
    )
    allowed = causal[None] & (doc_blk[:, :, None] == doc_blk[:, None, :])
    cumul_heads = jnp.swapaxes(cumulative, 1, 2)
    spread_log = jnp.where(
        allowed[:, None], cumul_heads[:, :, :, None] - cumul_heads[:, :, None, :], 0.0
    )
    decay_grid = jnp.where(allowed[:, None], jnp.exp(spread_log), 0.0)
    scores = jnp.einsum("gihd,gjhd->ghij", query_blk, key_blk, preferred_element_type=jnp.float32)
    weights = (scores * decay_grid).astype(jnp.bfloat16)
    inside = jnp.einsum("ghij,gjhd->gihd", weights, value_blk, preferred_element_type=jnp.float32)
    carried = (doc_blk == prior_doc[:, None]).astype(jnp.float32)
    leading = carried[:, :, None] * jnp.exp(cumulative)
    closing_doc = (doc_blk == doc_blk[:, -1:]).astype(jnp.float32)
    key_weight = closing_doc[:, :, None] * jnp.exp(cumulative[:, -1:, :] - cumulative)
    weighted = (key_blk.astype(jnp.float32) * key_weight[..., None]).astype(jnp.bfloat16)
    update = jnp.einsum("gjhd,gjhe->ghde", weighted, value_blk, preferred_element_type=jnp.float32)
    factor = carried[:, -1:] * jnp.exp(cumulative[:, -1, :])
    return (inside, leading, factor, update)


def span_pass(query_rows, key_rows, value_rows, decay_rows, documents, before):
    spans = query_rows.shape[0]
    per_step = math.gcd(spans, max(1, 32 // query_rows.shape[2]))

    def blocked(array):
        return array.reshape((spans // per_step, per_step) + array.shape[1:])

    pieces = lax.map(
        lambda batch_item: local_terms(*batch_item),
        tuple(
            (
                blocked(array)
                for array in (query_rows, key_rows, value_rows, decay_rows, documents, before)
            )
        ),
    )
    return tuple((array.reshape((spans,) + array.shape[2:]) for array in pieces))


def join_states(first_pair, second_pair):
    return (
        first_pair[0] * second_pair[0],
        second_pair[0][..., None, None] * first_pair[1] + second_pair[1],
    )


def prefix_states(factor, update):
    running_factor, running_update = lax.associative_scan(join_states, (factor, update), axis=0)
    prior_factor = jnp.concatenate([jnp.ones_like(factor[:1]), running_factor[:-1]], axis=0)
    prior_update = jnp.concatenate([jnp.zeros_like(update[:1]), running_update[:-1]], axis=0)
    return (prior_factor, prior_update, running_factor[-1], running_update[-1])


def with_state(query_rows, inside, leading, states):
    across = jnp.einsum(
        "nihd,nhde->nihe", query_rows.astype(jnp.float32), states, precision=lax.Precision.HIGHEST
    )
    return inside + across * leading[..., None]


def shards(queries, keys_in, values_in, log_decay, gate_logits, norm_gain, doc_lengths):
    local_len = queries.shape[0]
    spans = local_len // SPAN
    positions = lax.axis_index("seq") * local_len + lax.iota(jnp.int32, local_len)
    documents = doc_index(doc_lengths, positions).reshape(spans, SPAN)
    before = doc_index(doc_lengths, positions - 1).reshape(spans, SPAN)[:, 0]
    span_shape = (spans, SPAN, HEADS, HEAD_DIM)
    query_rows = queries.reshape(span_shape)
    key_rows = keys_in.reshape(span_shape)
    value_rows = values_in.reshape(span_shape)
    decay_rows = log_decay.astype(jnp.float32).reshape(spans, SPAN, HEADS)
    inside, leading, factor, update = span_pass(
        query_rows, key_rows, value_rows, decay_rows, documents, before
    )
    prior_factor, prior_update, device_factor, device_update = prefix_states(factor, update)
    owner_factor, owner_update = (
        lax.all_to_all(
            device_factor.reshape(1, HEADS), "seq", split_axis=1, concat_axis=0, tiled=True
        ),
        lax.all_to_all(
            device_update.reshape(1, HEADS, HEAD_DIM, HEAD_DIM),
            "seq",
            split_axis=1,
            concat_axis=0,
            tiled=True,
        ),
    )
    entry_factor, entry_update, total_factor, total_update = prefix_states(
        owner_factor, owner_update
    )
    incoming_update = lax.all_to_all(
        entry_update, "seq", split_axis=0, concat_axis=1, tiled=True
    ).reshape(HEADS, HEAD_DIM, HEAD_DIM)
    states = prior_factor[:, :, None, None] * incoming_update[None] + prior_update
    mixed = with_state(query_rows, inside, leading, states).reshape(local_len, HEADS * HEAD_DIM)
    inverse_rms = lax.rsqrt(jnp.mean(mixed * mixed, axis=1, keepdims=True) + EPS)
    gated = (
        mixed * inverse_rms * norm_gain[None, :] * jax.nn.sigmoid(gate_logits.astype(jnp.float32))
    )
    return (gated.astype(jnp.bfloat16), total_update)


def solution(mesh):
    in_specs = (
        P(("grp", "seq"), None),
        P(("grp", "seq"), None),
        P(("grp", "seq"), None),
        P(("grp", "seq"), None),
        P(("grp", "seq"), None),
        P(),
        P("grp"),
    )
    out_specs = (P(("grp", "seq"), None), P(("grp", "seq"), None, None))
    return jax.shard_map(shards, mesh=mesh, in_specs=in_specs, out_specs=out_specs, check_vma=False)
```

profile of v0, /device:TPU:13, one launch (start us, length us, event | category | flops | bytes accessed | tf_op | source)
XLA Modules:
  0.0 327.3 jit_solution(16462266262842617301)
XLA Ops:
  0.7 0.8 reduce-window.8
  1.5 0.1 convert_reduce_fusion
  1.6 0.5 slice.150
  2.1 0.6 slice.147
  4.0 0.2 fusion.25
  4.1 0.2 multiply_reduce_fusion.1
  4.3 0.7 mul.191
  5.0 6.5 %all-to-all-start.1 = ((f32[1,16,4]{2,0,1:T(1,128)}), f32[1,16,4]{2,0,1:T(1,128)S(1)}, u32[]{:S(2)}, u32[]{:S(2)}) async-start(f32[1,16,4]{2,0,1:T(1,128)} %bitcast.18), calls=%async_computation.1 | async-start | bytes 16384 | tf_op jit(solution)/shard_map/all_to_all | solution.py:104
  11.6 6.4 %copy.65 = bf16[256,8192]{0,1:T(8,128)(2,1)} copy(bf16[256,8192]{1,0:T(8,128)(2,1)} %param.8) | data formatting | bytes 8388608 | tf_op jit(solution)/shard_map/reshape.12
  17.9 1.2 compare_convert_fusion.1
  19.2 0.1 multiply_bitcast_fusion.1
  19.3 6.7 %fusion.17 = f32[1,64,128,128]{3,2,0,1:T(8,128)} fusion(bf16[256,64,128]{0,2,1:T(8,128)(2,1)} %bitcast.85, f32[256,64]{0,1:T(8,128)S(1)} %get-tuple-element.32, bf16[256,8192]{1,0:T(8,128)(2,1)} %param.9), kind=kOutput, calls=%fused_computation.19 | convolution fusion | flops 543162368 | bytes 12648448 | tf_op jit(solution)/shard_map/while/body/eval_jaxpr/gjhd,gjhe->ghde/dot_general | solution.py:43
  26.0 6.0 %all-to-all-start = ((f32[1,64,128,128]{3,2,0,1:T(8,128)}), f32[1,64,128,128]{3,2,0,1:T(8,128)}, u32[]{:S(2)}, u32[]{:S(2)}) async-start(f32[1,64,128,128]{3,2,0,1:T(8,128)} %fusion.17), calls=%async_computation | async-start | bytes 8388608 | tf_op jit(solution)/shard_map/all_to_all | solution.py:107
  32.0 0.1 copy.56
  32.1 0.1 slice.120
  32.2 0.1 slice.124
  32.3 0.1 slice.119
  32.4 0.1 copy.58
  32.4 0.1 slice.126
  32.5 0.1 slice.130
  32.6 0.1 slice.125
  32.7 0.1 copy.60
  32.8 0.1 slice.132
  32.9 0.1 slice.136
  33.0 0.1 copy.57
  33.1 0.1 copy.59
  33.2 0.1 copy.61
  33.3 0.2 slice_reduce_fusion.2
  33.5 0.2 slice_reduce_fusion.1
  33.7 90.8 %all-to-all-done = f32[1,64,128,128]{3,2,0,1:T(8,128)} async-done(((f32[1,64,128,128]{3,2,0,1:T(8,128)}), f32[1,64,128,128]{3,2,0,1:T(8,128)}, u32[]{:S(2)}, u32[]{:S(2)}) %all-to-all-start) | async-done | bytes 4194336 | tf_op jit(solution)/shard_map/all_to_all | solution.py:107
  124.5 1.0 slice_bitcast_fusion
  125.4 2.5 slice_add_fusion.1
  127.9 0.7 slice.152
  128.7 0.2 slice_add_fusion.2
  128.8 0.1 slice_add_fusion.3
  128.9 0.1 slice_add_fusion.4
  129.0 0.8 pad_add_fusion
  129.9 0.1 fusion.28
  130.0 0.9 pad_maximum_fusion.2
  130.8 3.5 %pad.28 = f32[4,4,128,128]{3,2,1,0:T(8,128)S(1)} pad(f32[2,4,128,128]{3,2,1,0:T(8,128)} %pad_maximum_fusion.2, f32[]{:T(128)} %constant.28.clone.1), padding=0_1_1x0_0_0x0_0_0x0_0_0 | pad | bytes 1572868 | tf_op jit(solution)/shard_map/pad | solution.py:75
  134.3 5.8 %pad.29 = f32[4,4,128,128]{3,2,1,0:T(8,128)} pad(f32[2,4,128,128]{3,2,1,0:T(8,128)} %pad_add_fusion, f32[]{:T(128)} %constant.28.clone.1), padding=1_0_1x0_0_0x0_0_0x0_0_0 | pad | bytes 1572868 | tf_op jit(solution)/shard_map/pad | solution.py:75
  140.1 2.4 add.96
  142.5 1.3 fusion.21
  143.8 0.1 pad_maximum_fusion.1
  143.9 6.3 %pad.30 = f32[8,4,128,128]{3,2,1,0:T(8,128)} pad(f32[4,4,128,128]{3,2,1,0:T(8,128)S(1)} %pad_maximum_fusion.1, f32[]{:T(128)} %constant.28.clone.1), padding=0_1_1x0_0_0x0_0_0x0_0_0 | pad | bytes 3145732 | tf_op jit(solution)/shard_map/pad | solution.py:75
  150.2 6.4 %pad.31 = f32[8,4,128,128]{3,2,1,0:T(8,128)} pad(f32[4,4,128,128]{3,2,1,0:T(8,128)S(1)} %copy-done.4, f32[]{:T(128)} %constant.28.clone.1), padding=1_0_1x0_0_0x0_0_0x0_0_0 | pad | bytes 3145732 | tf_op jit(solution)/shard_map/pad | solution.py:75
  156.6 2.6 add.98
  159.2 0.2 copy-done.2
  159.4 0.6 copy-done.3
  160.1 1.8 fusion.20
  161.9 1.5 pad_maximum_fusion
  163.4 18.4 %pad.32 = f32[16,4,128,128]{3,2,1,0:T(8,128)} pad(f32[8,4,128,128]{3,2,1,0:T(8,128)} %pad_maximum_fusion, f32[]{:T(128)} %constant.28.clone.1), padding=0_1_1x0_0_0x0_0_0x0_0_0 | pad | bytes 6291460 | tf_op jit(solution)/shard_map/pad | solution.py:75
  181.8 12.0 %pad.33 = f32[16,4,128,128]{3,2,1,0:T(8,128)} pad(f32[8,4,128,128]{3,2,1,0:T(8,128)S(1)} %add.98, f32[]{:T(128)} %constant.28.clone.1), padding=1_0_1x0_0_0x0_0_0x0_0_0 | pad | bytes 6291460 | tf_op jit(solution)/shard_map/pad | solution.py:75
  193.8 4.0 %slice_add_fusion = f32[15,4,128,128]{3,2,1,0:T(8,128)S(1)} fusion(f32[16,4,128,128]{3,2,1,0:T(8,128)} %pad.33, f32[16,4,128,128]{3,2,1,0:T(8,128)} %pad.32), kind=kLoop, calls=%fused_computation.14 | loop fusion | flops 983040 | bytes 11796480 | tf_op jit(solution)/shard_map/add | solution.py:75
  197.8 2.5 concatenate.15
  200.2 4.9 %all-to-all-start.2 = ((f32[16,4,128,128]{3,2,1,0:T(8,128)}), f32[16,4,128,128]{3,2,1,0:T(8,128)}, u32[]{:S(2)}, u32[]{:S(2)}) async-start(f32[16,4,128,128]{3,2,1,0:T(8,128)} %concatenate.15), calls=%async_computation.2 | async-start | bytes 8388608 | tf_op jit(solution)/shard_map/all_to_all | solution.py:118
  205.1 0.1 fusion.26
  205.3 11.7 %fusion.2 = f32[64,256,128]{1,2,0:T(8,128)} fusion(bf16[256,64,128]{0,2,1:T(8,128)(2,1)} %bitcast.86, f32[64,256]{1,0:T(8,128)S(1)} %bitcast.88, pred[256,256]{1,0:T(8,128)(4,1)S(1)} %fusion.26, bf16[256,8192]{1,0:T(8,128)(2,1)} %param.9, bf16[256,8192]{1,0:T(8,128)(2,1)} %param.7), kind=kOutput, calls=%fused_computation.7 | convolution fusion | flops 2168455168 | bytes 21102592 | tf_op jit(solution)/shard_map/while/body/eval_jaxpr/ghij,gjhd->gihd/dot_general | solution.py:37
  217.0 12.0 %pad.62 = f32[15,4,128,128]{3,2,1,0:T(8,128)} pad(f32[8,4,128,128]{3,2,1,0:T(8,128)S(1)} %add.98, f32[]{:T(128)} %constant.28.clone.1), padding=0_0_1x0_0_0x0_0_0x0_0_0 | pad | bytes 6029316
  229.0 1.7 add_bitcast_fusion
  230.7 66.9 %all-to-all-done.2 = f32[16,4,128,128]{3,2,1,0:T(8,128)} async-done(((f32[16,4,128,128]{3,2,1,0:T(8,128)}), f32[16,4,128,128]{3,2,1,0:T(8,128)}, u32[]{:S(2)}, u32[]{:S(2)}) %all-to-all-start.2) | async-done | bytes 4194336 | tf_op jit(solution)/shard_map/all_to_all | solution.py:118
  297.6 13.6 %multiply_reduce_fusion = (f32[256]{0:T(256)S(1)}, f32[1,256,64,128]{1,3,2,0:T(8,128)}) fusion(f32[256,64]{0,1:T(8,128)S(1)} %get-tuple-element.44, f32[64,128,128]{2,1,0:T(8,128)} %bitcast.33, f32[64,256,128]{1,2,0:T(8,128)} %fusion.2, bf16[256,8192]{1,0:T(8,128)(2,1)} %param.7), kind=kOutput, calls=%fused_computation.4 | convolution fusion | flops 3229613824 | bytes 25232384 | tf_op jit(solution)/shard_map/nihd,nhde->nihe/dot_general | solution.py:82
  311.3 8.9 %copy.64 = f32[256,8192]{1,0:T(8,128)} copy(f32[256,8192]{0,1:T(8,128)} %bitcast.84) | data formatting | bytes 16777216 | tf_op jit(solution)/shard_map/reshape | solution.py:122
  320.2 7.2 %multiply_convert_fusion.1 = bf16[256,8192]{1,0:T(8,128)(2,1)} fusion(bf16[256,8192]{1,0:T(8,128)(2,1)} %param.11, f32[256,8192]{1,0:T(8,128)} %copy.64, f32[8192]{0:T(1024)S(1)} %copy-done.8, f32[256]{0:T(256)S(1)} %add_rsqrt_fusion), kind=kLoop, calls=%fused_computation.3 | loop fusion | flops 16777216 | bytes 16811008 | tf_op jit(solution)/shard_map/convert_element_type | solution.py:127
  (22 shorter events, 0.1 us)
Async XLA Ops:
  0.6 3.3 %copy-start = (bf16[256,64]{0,1:T(8,128)(2,1)S(1)}, bf16[256,64]{0,1:T(8,128)(2,1)}, u32[]{:S(2)}) copy-start(bf16[256,64]{0,1:T(8,128)(2,1)} %param.10) | copy-start | bytes 98308
  4.1 15.0 %copy-start.6 = (f32[256,64]{0,1:T(8,128)}, f32[256,64]{0,1:T(8,128)S(1)}, u32[]{:S(2)}) copy-start(f32[256,64]{0,1:T(8,128)S(1)} %fusion.25) | copy-start | bytes 196612
  5.0 20.9 %all-to-all-start.1 = ((f32[1,16,4]{2,0,1:T(1,128)}), f32[1,16,4]{2,0,1:T(1,128)S(1)}, u32[]{:S(2)}, u32[]{:S(2)}) async-start(f32[1,16,4]{2,0,1:T(1,128)} %bitcast.18), calls=%async_computation.1 | async-start | bytes 16384 | tf_op jit(solution)/shard_map/all_to_all | solution.py:104
  26.0 98.5 %all-to-all-start = ((f32[1,64,128,128]{3,2,0,1:T(8,128)}), f32[1,64,128,128]{3,2,0,1:T(8,128)}, u32[]{:S(2)}, u32[]{:S(2)}) async-start(f32[1,64,128,128]{3,2,0,1:T(8,128)} %fusion.17), calls=%async_computation | async-start | bytes 8388608 | tf_op jit(solution)/shard_map/all_to_all | solution.py:107
  140.1 3.7 %copy-start.5 = (f32[1,4,128,128]{3,2,1,0:T(8,128)S(1)}, f32[1,4,128,128]{3,2,1,0:T(8,128)}, u32[]{:S(2)}) copy-start(f32[1,4,128,128]{3,2,1,0:T(8,128)} %slice.152) | copy-start | bytes 786436
  143.8 6.4 %copy-start.4 = (f32[4,4,128,128]{3,2,1,0:T(8,128)S(1)}, f32[4,4,128,128]{3,2,1,0:T(8,128)}, u32[]{:S(2)}) copy-start(f32[4,4,128,128]{3,2,1,0:T(8,128)} %add.96) | copy-start | bytes 3145732
  156.6 2.9 copy-start.2
  156.6 3.5 %copy-start.3 = (f32[8,4,128,128]{3,2,1,0:T(8,128)S(1)}, f32[8,4,128,128]{3,2,1,0:T(8,128)}, u32[]{:S(2)}) copy-start(f32[8,4,128,128]{3,2,1,0:T(8,128)} %pad.31) | copy-start | bytes 6291460
  200.2 5.0 %copy-start.7 = (f32[256,64]{0,1:T(8,128)S(1)}, f32[256,64]{0,1:T(8,128)}, u32[]{:S(2)}) copy-start(f32[256,64]{0,1:T(8,128)} %copy-done.6) | copy-start | bytes 196612
  200.2 97.4 %all-to-all-start.2 = ((f32[16,4,128,128]{3,2,1,0:T(8,128)}), f32[16,4,128,128]{3,2,1,0:T(8,128)}, u32[]{:S(2)}, u32[]{:S(2)}) async-start(f32[16,4,128,128]{3,2,1,0:T(8,128)} %concatenate.15), calls=%async_computation.2 | async-start | bytes 8388608 | tf_op jit(solution)/shard_map/all_to_all | solution.py:118
  311.3 8.9 %copy-start.8 = (f32[8192]{0:T(1024)S(1)}, f32[8192]{0:T(1024)}, u32[]{:S(2)}) copy-start(f32[8192]{0:T(1024)} %param.12) | copy-start | bytes 98308
  320.2 7.2 %copy-start.1 = (bf16[256,64]{0,1:T(8,128)(2,1)S(1)}, bf16[256,64]{0,1:T(8,128)(2,1)}, u32[]{:S(2)}) copy-start(bf16[256,64]{0,1:T(8,128)(2,1)} %param.10) | copy-start | bytes 98308
where the time goes:
time: 330 us; the launch traced here: 327 us
  waiting for transfers between devices  158 us (48%)
  local copies, waits for them, and re-layouts  88.2 us (27%)
  matrix products  32.2 us (10%)
  other arithmetic  29.8 us (9%)
  starting transfers between devices  17.5 us (5%)
    all_to_all x1, waiting for transfers between devices, shards(): lax.all_to_all(device_update.reshape(1, HEADS, HEAD_DIM, HEAD_DIM), 'seq'...  90.8 us
    all_to_all x1, waiting for transfers between devices, shards(): lax.all_to_all(entry_update, 'seq', split_axis=0, concat_axis=1, tiled=True)  66.9 us
    pad x6, local copies, waits for them, and re-layouts, prefix_states(): lax.associative_scan(join_states, (factor, update), axis=0)  52.3 us
    dot_general x1, matrix products, with_state(): jnp.einsum('nihd,nhde->nihe', query_rows.astype(jnp.float32), states, pre...  13.6 us
    unnamed x19, local copies, waits for them, and re-layouts  12.9 us
    dot_general x1, matrix products, local_terms(): jnp.einsum('ghij,gjhd->gihd', weights, value_blk, preferred_element_type=...  11.7 us
    add x4, other arithmetic, prefix_states(): lax.associative_scan(join_states, (factor, update), axis=0)  9.85 us
    reshape x1, local copies, waits for them, and re-layouts, shards(): with_state(query_rows, inside, leading, states)  8.91 us
  transfers between devices with their start and end apart: 3, of which 2 were waited for; matrix products, arithmetic and copies ran while one was open for 13% of the time, Pallas kernels for 0%

commit v1 on v0

v1 whole, which is shorter than its diff:
```python
import functools
import math

import jax
import jax.numpy as jnp
from jax import lax
from jax.experimental import pallas as pl
from jax.experimental.pallas import tpu as pltpu
from jax.sharding import PartitionSpec as P

EPS = 1e-05
D = 128
GROUP = 4
CHUNKS = 8
F32, BF16 = jnp.float32, jnp.bfloat16
MESH = pl.DeviceIdType.MESH


def dot(a, b, dims):
    return lax.dot_general(a, b, (dims, ((), ())), preferred_element_type=F32)


def kernel(
    n, heads, chunks,
    q_hbm, k_hbm, v_hbm, g_hbm, ld_ref, gain_ref, docs_ref,
    out_hbm, fin_ref,
    q_s, k_s, v_s, g_s, gate_s, mix_s, ssq_s, pen_s, cumt_s, cumc_s, kw_s, lead_s,
    fac_own, fac_s, u_own, u_core, u_mine, u_send, u_pair, s_in, s_out, e_send, e_half, x_send, ent, fin_s,
    load_sem, out_sem, fac_ss, fac_rs, core_ss, core_rs, pair_ss, pair_rs, z_ss, z_rs, e_ss, e_rs,
    x_ss, x_rs, f_ss, f_rs, f_ls,
):
    tok = q_hbm.shape[0]
    hc = heads // chunks
    half = hc // 2
    w = half // 2
    planes = n // GROUP
    hn = heads // n
    g = math.gcd(w, hn)
    me = lax.axis_index("seq")
    plane = me // GROUP
    r = me % GROUP
    y = r // 2
    c = r % 2
    core_peer = plane * GROUP + y * 2 + (1 - c)
    pair_peer = plane * GROUP + (1 - y) * 2 + c

    def send(src, dst, ss, rs, dev):
        return pltpu.make_async_remote_copy(
            src_ref=src, dst_ref=dst, send_sem=ss, recv_sem=rs,
            device_id={"seq": dev}, device_id_type=MESH,
        )

    barrier = pltpu.get_barrier_semaphore()

    def greet(i, carry):
        pl.semaphore_signal(barrier, inc=1, device_id={"seq": (me + i) % n}, device_id_type=MESH)
        return carry

    lax.fori_loop(1, n, greet, 0)

    def cols(j):
        return pl.ds(pl.multiple_of(j * (hc * D), hc * D), hc * D)

    def load(which, hbm, vm, j):
        return pltpu.make_async_copy(hbm.at[:, cols(j)], vm.at[:, cols(j)], load_sem.at[which, j])

    loads = ((k_hbm, k_s), (v_hbm, v_s), (q_hbm, q_s), (g_hbm, g_s))

    def start_kv(j, carry):
        load(0, k_hbm, k_s, j).start()
        load(1, v_hbm, v_s, j).start()
        return carry

    def start_qg(j, carry):
        load(2, q_hbm, q_s, j).start()
        load(3, g_hbm, g_s, j).start()
        return carry

    lax.fori_loop(0, chunks, start_kv, 0)
    lax.fori_loop(0, chunks, start_qg, 0)

    n_docs = docs_ref.shape[0]
    rows = lax.broadcasted_iota(jnp.int32, (tok, tok), 0)
    lanes = lax.broadcasted_iota(jnp.int32, (tok, tok), 1)
    base = me * tok
    doc_col = jnp.zeros((tok, tok), jnp.int32)
    doc_row = jnp.zeros((tok, tok), jnp.int32)
    before = jnp.int32(0)
    last = jnp.int32(0)
    end = jnp.int32(0)
    for d in range(n_docs):
        end = end + docs_ref[d]
        doc_col = doc_col + jnp.where(rows + base >= end, 1, 0)
        doc_row = doc_row + jnp.where(lanes + base >= end, 1, 0)
        before = before + jnp.where(base - 1 >= end, 1, 0)
        last = last + jnp.where(base + tok - 1 >= end, 1, 0)
    causal = rows >= lanes
    pen_s[...] = jnp.where(causal & (doc_col == doc_row), 0.0, -1e30).astype(F32)
    tri = jnp.where(causal, 1.0, 0.0).astype(BF16)
    ld = ld_ref[...]
    cum = dot(tri, ld, ((1,), (0,)))
    cumt = dot(ld, tri, ((0,), (1,)))
    cumt_s[...] = cumt
    carried = jnp.where(doc_col[:, :heads] == before, 1.0, 0.0).astype(F32)
    closing = jnp.where(doc_col[:, :heads] == last, 1.0, 0.0).astype(F32)
    lead = carried * jnp.exp(cum)
    kw = closing * jnp.exp(cum[tok - 1:tok, :] - cum)
    for j in range(chunks):
        at = slice(j * hc, (j + 1) * hc)
        cumc_s[j] = cum[:, at]
        lead_s[j] = lead[:, at]
        kw_s[j] = kw[:, at]
    own_f = jnp.where(last == before, 1.0, 0.0).astype(F32) * jnp.exp(
        jnp.broadcast_to(cumt[:, tok - 1:tok], (heads, D))
    )
    fac_own[...] = own_f
    fac_s[r] = own_f

    @pl.when(plane == 0)
    def _():
        s_in[...] = jnp.zeros_like(s_in)

    def lane(t):
        return slice(t * D, (t + 1) * D)

    def hcol(j, t):
        return pl.ds(pl.multiple_of(j * (hc * D) + t * D, D), D)

    def updates(j):
        load(0, k_hbm, k_s, j).wait()
        load(1, v_hbm, v_s, j).wait()
        kwj = kw_s[j]
        for t in range(hc):
            kk = k_s[:, hcol(j, t)].astype(F32)
            wk = (kk * kwj[:, t:t + 1]).astype(BF16)
            up = dot(wk, v_s[:, hcol(j, t)], ((0,), (0,)))
            u_own[j, t // half, (t % half) // w, t % w] = up.astype(BF16)

    def frow(slot, h):
        return fac_s[slot, pl.ds(h, 1), :]

    def core_copy(j):
        return send(u_own.at[j, 1 - c], u_core.at[j], core_ss.at[j], core_rs.at[j], core_peer)

    def pair_copy(j):
        return send(u_send.at[j], u_pair.at[j], pair_ss.at[j], pair_rs.at[j], pair_peer)

    def combine(j):
        core_copy(j).wait_recv()
        for k in range(w):
            for mine in (True, False):
                yo = y if mine else 1 - y
                h = j * hc + c * half + yo * w + k
                f1 = frow(2 * y + 1, h)
                fa = jnp.where(c == 0, f1, 1.0)
                fb = jnp.where(c == 0, 1.0, f1)
                val = fa * u_own[j, c, yo, k].astype(F32) + fb * u_core[j, yo, k].astype(F32)
                if mine:
                    u_mine[j, k] = val
                else:
                    u_send[j, k] = val.astype(BF16)
        pair_copy(j).start()

    def z_copy(j):
        return send(s_out.at[j], s_in.at[j], z_ss.at[j], z_rs.at[j], (me + GROUP) % n)

    def e_copy(j):
        return send(e_send.at[j], e_half.at[j, y], e_ss.at[j], e_rs.at[j], pair_peer)

    def fin_place(j, s):
        h0 = j * hc + c * half + y * w + s * g
        return h0 // hn, h0 % hn

    def fin_copy(j, s):
        dev, off = fin_place(j, s)
        return send(
            s_out.at[j, pl.ds(s * g, g)], fin_s.at[pl.ds(off, g)],
            f_ss.at[j, s], f_rs.at[off // g], dev,
        )

    def fin_local(j, s):
        _, off = fin_place(j, s)
        return pltpu.make_async_copy(s_out.at[j, pl.ds(s * g, g)], fin_s.at[pl.ds(off, g)], f_ls)

    def chain(j):
        pair_copy(j).wait_recv()

        @pl.when(plane > 0)
        def _():
            z_copy(j).wait_recv()

        for k in range(w):
            h = j * hc + c * half + y * w + k
            f01 = frow(0, h) * frow(1, h)
            f23 = frow(2, h) * frow(3, h)
            mine = u_mine[j, k]
            other = u_pair[j, k].astype(F32)
            entry = s_in[j, k].astype(F32)
            mid = f01 * entry + jnp.where(y == 0, mine, other)
            s_out[j, k] = (f23 * mid + jnp.where(y == 0, other, mine)).astype(BF16)
            e_send[j, k] = jnp.where(y == 0, mid, entry).astype(BF16)
            e_half[j, y, k] = jnp.where(y == 0, entry, mid).astype(BF16)

        @pl.when(plane < planes - 1)
        def _():
            z_copy(j).start()

        e_copy(j).start()

        @pl.when(plane == planes - 1)
        def _():
            for s in range(w // g):
                dev, _off = fin_place(j, s)

                @pl.when(dev != me)
                def _():
                    fin_copy(j, s).start()

                @pl.when(dev == me)
                def _():
                    fin_local(j, s).start()
                    fin_local(j, s).wait()

    def inside(j):
        load(2, q_hbm, q_s, j).wait()
        load(3, g_hbm, g_s, j).wait()
        cj = cumc_s[j]
        blk = tok // 2
        for t in range(hc):
            row = cumt_s[pl.ds(j * hc + t, 1), :]
            for b in range(2):
                at = slice(b * blk, (b + 1) * blk)
                width = (b + 1) * blk
                scores = dot(q_s[at, hcol(j, t)], k_s[:width, hcol(j, t)], ((1,), (1,)))
                grid = jnp.exp((cj[at, t:t + 1] - row[:, :width]) + pen_s[at, :width])
                wt = (scores * grid).astype(BF16)
                mix_s[at, hcol(j, t)] = dot(wt, v_s[:width, hcol(j, t)], ((1,), (0,)))
            gate = g_s[:, hcol(j, t)].astype(F32)
            gate_s[:, hcol(j, t)] = gain_ref[:, hcol(j, t)] * jax.nn.sigmoid(gate)

    def x_copy(j):
        return send(x_send.at[j], ent.at[j, c], x_ss.at[j], x_rs.at[j], core_peer)

    def spread(j):
        e_copy(j).wait_recv()
        for yo in range(2):
            for k in range(w):
                h = j * hc + c * half + yo * w + k
                first = e_half[j, yo, k]
                u0 = jnp.where(c == 0, u_own[j, 0, yo, k], u_core[j, yo, k]).astype(F32)
                second = (frow(2 * y, h) * first.astype(F32) + u0).astype(BF16)
                ent[j, c, yo, k] = jnp.where(c == 0, first, second)
                x_send[j, yo, k] = jnp.where(c == 0, second, first)
        x_copy(j).start()

    def across(j):
        x_copy(j).wait_recv()
        lj = lead_s[j]
        acc = ssq_s[...]
        for t in range(hc):
            st = ent[j, t // half, (t % half) // w, t % w]
            mixed = mix_s[:, hcol(j, t)] + lj[:, t:t + 1] * dot(q_s[:, hcol(j, t)], st, ((1,), (0,)))
            acc = acc + mixed * mixed
            mix_s[:, hcol(j, t)] = mixed * gate_s[:, hcol(j, t)]
        ssq_s[...] = acc

    def fac_copy(d):
        return send(fac_own, fac_s.at[r], fac_ss.at[d - 1], fac_rs.at[d - 1], plane * GROUP + (r + d) % GROUP)

    updates(0)
    pl.semaphore_wait(barrier, n - 1)
    for d in range(1, GROUP):
        fac_copy(d).start()
    core_copy(0).start()
    ssq_s[...] = jnp.zeros_like(ssq_s)
    for d in range(1, GROUP):
        fac_copy(d).wait_recv()

    def first_pass(j, carry):
        updates(j)
        core_copy(j).start()
        combine(j - 1)
        return carry

    lax.fori_loop(1, chunks, first_pass, 0)
    combine(chunks - 1)

    def second_pass(j, carry):
        inside(j)
        chain(j)
        return carry

    lax.fori_loop(0, chunks, second_pass, 0)
    spread(0)

    def third_pass(j, carry):
        spread(j)
        across(j - 1)
        return carry

    lax.fori_loop(1, chunks, third_pass, 0)
    across(chunks - 1)

    inv = lax.rsqrt(jnp.sum(ssq_s[...], axis=1, keepdims=True) * (1.0 / (heads * D)) + EPS)

    def store(j):
        return pltpu.make_async_copy(g_s.at[:, cols(j)], out_hbm.at[:, cols(j)], out_sem.at[j])

    def finish(j, carry):
        for t in range(hc):
            g_s[:, hcol(j, t)] = (mix_s[:, hcol(j, t)] * inv).astype(BF16)
        store(j).start()
        return carry

    lax.fori_loop(0, chunks, finish, 0)

    for s in range(hn // g):
        h0 = me * hn + s * g
        pos = h0 % hc
        src = (planes - 1) * GROUP + ((pos % half) // w) * 2 + pos // half

        @pl.when(src != me)
        def _():
            send(
                s_out.at[0, pl.ds(0, g)], fin_s.at[pl.ds(s * g, g)], f_ss.at[0, 0], f_rs.at[s], core_peer
            ).wait_recv()

    fin_ref[...] = fin_s[...].astype(F32)

    for d in range(1, GROUP):
        fac_copy(d).wait_send()

    def drain(j, carry):
        core_copy(j).wait_send()
        pair_copy(j).wait_send()
        e_copy(j).wait_send()
        x_copy(j).wait_send()
        store(j).wait()

        @pl.when(plane < planes - 1)
        def _():
            z_copy(j).wait_send()

        @pl.when(plane == planes - 1)
        def _():
            for s in range(w // g):
                dev, _off = fin_place(j, s)

                @pl.when(dev != me)
                def _():
                    fin_copy(j, s).wait_send()

        return carry

    lax.fori_loop(0, chunks, drain, 0)


def shards(n, queries, keys_in, values_in, log_decay, gate_logits, norm_gain, doc_lengths):
    tok, width = queries.shape
    heads = width // D
    chunks = CHUNKS
    hc = heads // chunks
    half = hc // 2
    w = half // 2
    hn = heads // n
    g = math.gcd(w, hn)
    vm = pltpu.VMEM
    dma = pltpu.SemaphoreType.DMA
    anyspace = pl.BlockSpec(memory_space=pl.ANY)
    vspec = pl.BlockSpec(memory_space=pltpu.VMEM)
    part = vm((chunks, w, D, D), BF16)
    scratch = [
        vm((tok, width), BF16), vm((tok, width), BF16), vm((tok, width), BF16), vm((tok, width), BF16),
        vm((tok, width), F32), vm((tok, width), F32), vm((tok, D), F32), vm((tok, tok), F32),
        vm((heads, tok), F32), vm((chunks, tok, hc), F32), vm((chunks, tok, hc), F32), vm((chunks, tok, hc), F32),
        vm((heads, D), F32), vm((GROUP, heads, D), F32),
        vm((chunks, 2, 2, w, D, D), BF16), vm((chunks, 2, w, D, D), BF16), vm((chunks, w, D, D), F32),
        part, part, part, part, part,
        vm((chunks, 2, w, D, D), BF16), vm((chunks, 2, w, D, D), BF16),
        vm((chunks, 2, 2, w, D, D), BF16), vm((hn, D, D), BF16),
        dma((4, chunks)), dma((chunks,)), dma((GROUP - 1,)), dma((GROUP - 1,)),
        dma((chunks,)), dma((chunks,)), dma((chunks,)), dma((chunks,)), dma((chunks,)), dma((chunks,)),
        dma((chunks,)), dma((chunks,)), dma((chunks,)), dma((chunks,)),
        dma((chunks, w // g)), dma((hn // g,)), dma,
    ]
    return pl.pallas_call(
        functools.partial(kernel, n, heads, chunks),
        out_shape=(
            jax.ShapeDtypeStruct((tok, width), BF16),
            jax.ShapeDtypeStruct((hn, D, D), F32),
        ),
        in_specs=[anyspace] * 4 + [vspec, vspec, pl.BlockSpec(memory_space=pltpu.SMEM)],
        out_specs=(anyspace, vspec),
        scratch_shapes=scratch,
        compiler_params=pltpu.CompilerParams(
            collective_id=0, has_side_effects=True, vmem_limit_bytes=60 * 1024 * 1024
        ),
    )(queries, keys_in, values_in, gate_logits, log_decay, norm_gain.reshape(1, width), doc_lengths)


def solution(mesh):
    rows = P(("grp", "seq"), None)
    return jax.shard_map(
        functools.partial(shards, mesh.shape["seq"]),
        mesh=mesh,
        in_specs=(rows, rows, rows, rows, rows, P(), P("grp")),
        out_specs=(rows, P(("grp", "seq"), None, None)),
        check_vma=False,
    )
```

time: 330 us -> 60.5 us (0.18)
  the two profiles are of different devices: /device:TPU:13 before, /device:TPU:25 now
where the time goes in v1:
time: 60.5 us; the launch traced here: 60.3 us
  Pallas kernels  52.8 us (87%)
  local copies, waits for them, and re-layouts  6.88 us (11%)
  between operations  0.65 us (1%)
    pallas_call x1, Pallas kernels, shards(): pl.pallas_call(functools.partial(kernel, n, heads, chunks), out_shape=(ja...  52.8 us
    unnamed x5, local copies, waits for them, and re-layouts  6.88 us

profile of v1, /device:TPU:25, one launch (start us, length us, event | category | flops | bytes accessed | tf_op | source)
XLA Modules:
  0.0 60.3 jit_solution(885334218239332412)
XLA Ops:
  0.6 1.5 %copy.9.ld_ref = bf16[256,64]{1,0:T(8,128)(2,1)} copy(bf16[256,64]{0,1:T(8,128)(2,1)} %param.10) | data formatting | bytes 65536 | tf_op args[3]
  2.1 52.8 %shard_map.86 = (bf16[256,8192]{1,0:T(8,128)(2,1)}, f32[4,128,128]{2,1,0:T(8,128)}) custom-call(bf16[256,8192]{1,0:T(8,128)(2,1)} %q_hbm.1, bf16[256,8192]{1,0:T(8,128)(2,1)} %k_hbm.1, bf16[256,8192]{1,0:T(8,128)(2,1)} %v_hbm.1, bf16[256,8192]{1,0:T(8,128)(2,1)} %g_hbm.1, bf16[256,64]{1,0:T(8,128)(2,1)} %copy.9.ld_ref, f32[1,8192]{1,0:T(1,128)} %bitcast.1, ...), custom_call_target="tpu_custom_call" | custom-call | tf_op jit(solution)/shard_map/pallas_call | solution.py:386
  54.9 0.0 copy-start
  54.9 4.7 %copy.12 = bf16[256,8192]{1,0:T(8,128)(2,1)} copy(bf16[256,8192]{1,0:T(8,128)(2,1)} %get-tuple-element.4) | data formatting | bytes 8388608
  59.6 0.0 copy-done
  59.6 0.7 %copy.13 = f32[4,128,128]{2,1,0:T(8,128)} copy(f32[4,128,128]{2,1,0:T(8,128)S(1)} %copy-done) | data formatting | bytes 524288
Async XLA Ops:
  54.9 4.7 %copy-start = (f32[4,128,128]{2,1,0:T(8,128)S(1)}, f32[4,128,128]{2,1,0:T(8,128)}, u32[]{:S(2)}) copy-start(f32[4,128,128]{2,1,0:T(8,128)} %get-tuple-element.5) | copy-start | bytes 786436

commit v2 on v1

--- a/solution.py
+++ b/solution.py
@@ -9,9 +9,16 @@
 from jax.sharding import PartitionSpec as P
 
 EPS = 1e-05
+LOG2E = 1.4426950408889634
 D = 128
 GROUP = 4
 CHUNKS = 8
+INSIDE_LAG = 2
+CHAIN_LAG = 4
+HOP_LAG = 2
+E_LAG = 4
+X_LAG = 2
+FINISH_PARTS = 4
 F32, BF16 = jnp.float32, jnp.bfloat16
 MESH = pl.DeviceIdType.MESH
 
@@ -23,9 +30,9 @@
 def kernel(
     n, heads, chunks,
     q_hbm, k_hbm, v_hbm, g_hbm, ld_ref, gain_ref, docs_ref,
-    out_hbm, fin_ref,
-    q_s, k_s, v_s, g_s, gate_s, mix_s, ssq_s, pen_s, cumt_s, cumc_s, kw_s, lead_s,
-    fac_own, fac_s, u_own, u_core, u_mine, u_send, u_pair, s_in, s_out, e_send, e_half, x_send, ent, fin_s,
+    mix_hbm, ssq_s, fin_s,
+    mix_s, q_s, k_s, v_s, g_s, pen_s, cumt_s, cumc_s, coef_s,
+    fac_own, fac_s, u_own, u_core, u_mine, u_send, u_pair, s_in, s_out, e_send, e_half, x_send, ent,
     load_sem, out_sem, fac_ss, fac_rs, core_ss, core_rs, pair_ss, pair_rs, z_ss, z_rs, e_ss, e_rs,
     x_ss, x_rs, f_ss, f_rs, f_ls,
 ):
@@ -98,18 +105,19 @@
     pen_s[...] = jnp.where(causal & (doc_col == doc_row), 0.0, -1e30).astype(F32)
     tri = jnp.where(causal, 1.0, 0.0).astype(BF16)
     ld = ld_ref[...]
-    cum = dot(tri, ld, ((1,), (0,)))
-    cumt = dot(ld, tri, ((0,), (1,)))
-    cumt_s[...] = cumt
+    cum = dot(tri, ld, ((1,), (1,)))
+    cumt = dot(ld, tri, ((1,), (1,)))
+    cumt_s[...] = LOG2E * cumt
     carried = jnp.where(doc_col[:, :heads] == before, 1.0, 0.0).astype(F32)
     closing = jnp.where(doc_col[:, :heads] == last, 1.0, 0.0).astype(F32)
     lead = carried * jnp.exp(cum)
     kw = closing * jnp.exp(cum[tok - 1:tok, :] - cum)
     for j in range(chunks):
         at = slice(j * hc, (j + 1) * hc)
-        cumc_s[j] = cum[:, at]
-        lead_s[j] = lead[:, at]
-        kw_s[j] = kw[:, at]
+        coef_s[j, :, 0:hc] = lead[:, at]
+        coef_s[j, :, hc:2 * hc] = kw[:, at]
+    for i in range(2 * chunks):
+        cumc_s[i] = LOG2E * cum[:, i * half:(i + 1) * half]
     own_f = jnp.where(last == before, 1.0, 0.0).astype(F32) * jnp.exp(
         jnp.broadcast_to(cumt[:, tok - 1:tok], (heads, D))
     )
@@ -129,7 +137,7 @@
     def updates(j):
         load(0, k_hbm, k_s, j).wait()
         load(1, v_hbm, v_s, j).wait()
-        kwj = kw_s[j]
+        kwj = coef_s[j, :, hc:2 * hc]
         for t in range(hc):
             kk = k_s[:, hcol(j, t)].astype(F32)
             wk = (kk * kwj[:, t:t + 1]).astype(BF16)
@@ -205,8 +213,6 @@
         def _():
             z_copy(j).start()
 
-        e_copy(j).start()
-
         @pl.when(plane == planes - 1)
         def _():
             for s in range(w // g):
@@ -221,22 +227,26 @@
                     fin_local(j, s).start()
                     fin_local(j, s).wait()
 
-    def inside(j):
-        load(2, q_hbm, q_s, j).wait()
-        load(3, g_hbm, g_s, j).wait()
-        cj = cumc_s[j]
+    def inside(i):
+        j = i // 2
+
+        @pl.when(i % 2 == 0)
+        def _():
+            load(2, q_hbm, q_s, j).wait()
+
+        ci = cumc_s[i]
         blk = tok // 2
-        for t in range(hc):
-            row = cumt_s[pl.ds(j * hc + t, 1), :]
-            for b in range(2):
-                at = slice(b * blk, (b + 1) * blk)
-                width = (b + 1) * blk
-                scores = dot(q_s[at, hcol(j, t)], k_s[:width, hcol(j, t)], ((1,), (1,)))
-                grid = jnp.exp((cj[at, t:t + 1] - row[:, :width]) + pen_s[at, :width])
-                wt = (scores * grid).astype(BF16)
-                mix_s[at, hcol(j, t)] = dot(wt, v_s[:width, hcol(j, t)], ((1,), (0,)))
-            gate = g_s[:, hcol(j, t)].astype(F32)
-            gate_s[:, hcol(j, t)] = gain_ref[:, hcol(j, t)] * jax.nn.sigmoid(gate)
+
+        for t in range(half):
+            at_h = pl.ds(pl.multiple_of(i * (half * D) + t * D, D), D)
+            row = cumt_s[pl.ds(i * half + t, 1), :]
+            scores = dot(q_s[:, at_h], k_s[:, at_h], ((1,), (1,)))
+            low = ci[:blk, t:t + 1] - row[:, :blk]
+            top = (scores[:blk, :blk] * jnp.exp2(low + pen_s[:blk, :blk])).astype(BF16)
+            bot = (scores[blk:] * jnp.exp2((ci[blk:, t:t + 1] - row) + pen_s[blk:, :])).astype(BF16)
+            top = jnp.concatenate([top, jnp.zeros_like(top)], axis=1)
+            wt = jnp.concatenate([top, bot], axis=0)
+            mix_s[:, at_h] = dot(wt, v_s[:, at_h], ((1,), (0,)))
 
     def x_copy(j):
         return send(x_send.at[j], ent.at[j, c], x_ss.at[j], x_rs.at[j], core_peer)
@@ -253,16 +263,22 @@
                 x_send[j, yo, k] = jnp.where(c == 0, second, first)
         x_copy(j).start()
 
+    def store(j):
+        return pltpu.make_async_copy(mix_s.at[:, cols(j)], mix_hbm.at[:, cols(j)], out_sem.at[j])
+
     def across(j):
         x_copy(j).wait_recv()
-        lj = lead_s[j]
+        load(3, g_hbm, g_s, j).wait()
+        lj = coef_s[j, :, 0:hc]
         acc = ssq_s[...]
         for t in range(hc):
             st = ent[j, t // half, (t % half) // w, t % w]
             mixed = mix_s[:, hcol(j, t)] + lj[:, t:t + 1] * dot(q_s[:, hcol(j, t)], st, ((1,), (0,)))
             acc = acc + mixed * mixed
-            mix_s[:, hcol(j, t)] = mixed * gate_s[:, hcol(j, t)]
+            gate = g_s[:, hcol(j, t)].astype(F32)
+            mix_s[:, hcol(j, t)] = mixed * (gain_ref[:, hcol(j, t)] * jax.nn.sigmoid(gate))
         ssq_s[...] = acc
+        store(j).start()
 
     def fac_copy(d):
         return send(fac_own, fac_s.at[r], fac_ss.at[d - 1], fac_rs.at[d - 1], plane * GROUP + (r + d) % GROUP)
@@ -273,46 +289,41 @@
         fac_copy(d).start()
     core_copy(0).start()
     ssq_s[...] = jnp.zeros_like(ssq_s)
+    updates(1)
+    core_copy(1).start()
     for d in range(1, GROUP):
         fac_copy(d).wait_recv()
-
-    def first_pass(j, carry):
-        updates(j)
-        core_copy(j).start()
-        combine(j - 1)
+    combine(0)
+
+    chain_lag = CHAIN_LAG + HOP_LAG * plane
+    e_lag = CHAIN_LAG + HOP_LAG * (planes - 1)
+    spread_lag = e_lag + E_LAG
+    across_lag = spread_lag + X_LAG
+    steps = max(chunks + across_lag, 2 * chunks + INSIDE_LAG)
+
+    def step(t, carry):
+        def at(lag, count, body):
+            @pl.when((t >= lag) & (t < lag + count))
+            def _():
+                body(t - lag)
+
+        def first(j):
+            updates(j)
+            core_copy(j).start()
+
+        at(1, chunks, combine)
+        at(chain_lag, chunks, chain)
+        at(e_lag, chunks, lambda j: e_copy(j).start())
+        at(spread_lag, chunks, spread)
+        at(0, chunks, first)
+        at(INSIDE_LAG, 2 * chunks, inside)
+        at(across_lag, chunks, across)
         return carry
 
-    lax.fori_loop(1, chunks, first_pass, 0)
-    combine(chunks - 1)
-
-    def second_pass(j, carry):
-        inside(j)
-        chain(j)
-        return carry
-
-    lax.fori_loop(0, chunks, second_pass, 0)
-    spread(0)
-
-    def third_pass(j, carry):
-        spread(j)
-        across(j - 1)
-        return carry
-
-    lax.fori_loop(1, chunks, third_pass, 0)
-    across(chunks - 1)
-
-    inv = lax.rsqrt(jnp.sum(ssq_s[...], axis=1, keepdims=True) * (1.0 / (heads * D)) + EPS)
-
-    def store(j):
-        return pltpu.make_async_copy(g_s.at[:, cols(j)], out_hbm.at[:, cols(j)], out_sem.at[j])
-
-    def finish(j, carry):
-        for t in range(hc):
-            g_s[:, hcol(j, t)] = (mix_s[:, hcol(j, t)] * inv).astype(BF16)
-        store(j).start()
-        return carry
-
-    lax.fori_loop(0, chunks, finish, 0)
+    lax.fori_loop(2, steps, step, 0)
+
+    total = jnp.sum(ssq_s[...], axis=1, keepdims=True) * (1.0 / (heads * D))
+    ssq_s[...] = jnp.broadcast_to(lax.rsqrt(total + EPS), (tok, D))
 
     for s in range(hn // g):
         h0 = me * hn + s * g
@@ -324,8 +335,6 @@
             send(
                 s_out.at[0, pl.ds(0, g)], fin_s.at[pl.ds(s * g, g)], f_ss.at[0, 0], f_rs.at[s], core_peer
             ).wait_recv()
-
-    fin_ref[...] = fin_s[...].astype(F32)
 
     for d in range(1, GROUP):
         fac_copy(d).wait_send()
@@ -353,6 +362,14 @@
         return carry
 
     lax.fori_loop(0, chunks, drain, 0)
+
+
+def finish_kernel(mix_ref, inv_ref, fin_in, out_ref, fin_ref):
+    inv = inv_ref[...]
+    for t in range(mix_ref.shape[1] // D):
+        at = slice(t * D, (t + 1) * D)
+        out_ref[:, at] = (mix_ref[:, at] * inv).astype(BF16)
+    fin_ref[...] = fin_in[...].astype(F32)
 
 
 def shards(n, queries, keys_in, values_in, log_decay, gate_logits, norm_gain, doc_lengths):
@@ -370,32 +387,53 @@
     vspec = pl.BlockSpec(memory_space=pltpu.VMEM)
     part = vm((chunks, w, D, D), BF16)
     scratch = [
+        vm((tok, width), F32),
         vm((tok, width), BF16), vm((tok, width), BF16), vm((tok, width), BF16), vm((tok, width), BF16),
-        vm((tok, width), F32), vm((tok, width), F32), vm((tok, D), F32), vm((tok, tok), F32),
-        vm((heads, tok), F32), vm((chunks, tok, hc), F32), vm((chunks, tok, hc), F32), vm((chunks, tok, hc), F32),
+        vm((tok, tok), F32),
+        vm((heads, tok), F32), vm((2 * chunks, tok, half), F32), vm((chunks, tok, 2 * hc), F32),
         vm((heads, D), F32), vm((GROUP, heads, D), F32),
         vm((chunks, 2, 2, w, D, D), BF16), vm((chunks, 2, w, D, D), BF16), vm((chunks, w, D, D), F32),
         part, part, part, part, part,
         vm((chunks, 2, w, D, D), BF16), vm((chunks, 2, w, D, D), BF16),
-        vm((chunks, 2, 2, w, D, D), BF16), vm((hn, D, D), BF16),
+        vm((chunks, 2, 2, w, D, D), BF16),
         dma((4, chunks)), dma((chunks,)), dma((GROUP - 1,)), dma((GROUP - 1,)),
         dma((chunks,)), dma((chunks,)), dma((chunks,)), dma((chunks,)), dma((chunks,)), dma((chunks,)),
         dma((chunks,)), dma((chunks,)), dma((chunks,)), dma((chunks,)),
         dma((chunks, w // g)), dma((hn // g,)), dma,
     ]
+    mixed, squares, final = pl.pallas_call(
+        functools.partial(kernel, n, heads, chunks),
+        out_shape=(
+            jax.ShapeDtypeStruct((tok, width), F32),
+            jax.ShapeDtypeStruct((tok, D), F32),
+            jax.ShapeDtypeStruct((hn, D, D), BF16),
+        ),
+        in_specs=[anyspace] * 4 + [vspec, vspec, pl.BlockSpec(memory_space=pltpu.SMEM)],
+        out_specs=(anyspace, vspec, vspec),
+        scratch_shapes=scratch,
+        compiler_params=pltpu.CompilerParams(
+            collective_id=0, has_side_effects=True, vmem_limit_bytes=60 * 1024 * 1024
+        ),
+    )(queries, keys_in, values_in, gate_logits, log_decay.T, norm_gain.reshape(1, width), doc_lengths)
+    rows = tok // FINISH_PARTS
     return pl.pallas_call(
-        functools.partial(kernel, n, heads, chunks),
+        finish_kernel,
         out_shape=(
             jax.ShapeDtypeStruct((tok, width), BF16),
             jax.ShapeDtypeStruct((hn, D, D), F32),
         ),
-        in_specs=[anyspace] * 4 + [vspec, vspec, pl.BlockSpec(memory_space=pltpu.SMEM)],
-        out_specs=(anyspace, vspec),
-        scratch_shapes=scratch,
-        compiler_params=pltpu.CompilerParams(
-            collective_id=0, has_side_effects=True, vmem_limit_bytes=60 * 1024 * 1024
+        grid=(FINISH_PARTS,),
+        in_specs=[
+            pl.BlockSpec((rows, width), lambda i: (i, 0)),
+            pl.BlockSpec((rows, D), lambda i: (i, 0)),
+            pl.BlockSpec((hn, D, D), lambda i: (0, 0, 0)),
+        ],
+        out_specs=(
+            pl.BlockSpec((rows, width), lambda i: (i, 0)),
+            pl.BlockSpec((hn, D, D), lambda i: (0, 0, 0)),
         ),
-    )(queries, keys_in, values_in, gate_logits, log_decay, norm_gain.reshape(1, width), doc_lengths)
+        compiler_params=pltpu.CompilerParams(vmem_limit_bytes=60 * 1024 * 1024),
+    )(mixed, squares, final)
 
 
 def solution(mesh):

time: 60.5 us -> 51.5 us (0.85)
  local copies, waits for them, and re-layouts: 6.88 us -> 0 us
  Pallas kernels: 52.8 us -> 50.5 us
    pallas_call x1, Pallas kernels: 52.8 us -> 44.5 us  [shards(): pl.pallas_call(functools.partial(kernel, n, heads, chunks), out_shape=(ja...]
    unnamed x5 -> x0, local copies, waits for them, and re-layouts: 6.88 us -> none
    pallas_call x0 -> x1, Pallas kernels: none -> 6.06 us  [shards(): pl.pallas_call(finish_kernel, out_shape=(jax.ShapeDtypeStruct((tok, width...]
where the time goes in v2:
time: 51.5 us; the launch traced here: 51.2 us
  Pallas kernels  50.5 us (98%)
  between operations  0.64 us (1%)
    pallas_call x1, Pallas kernels, shards(): pl.pallas_call(functools.partial(kernel, n, heads, chunks), out_shape=(ja...  44.5 us
    pallas_call x1, Pallas kernels, shards(): pl.pallas_call(finish_kernel, out_shape=(jax.ShapeDtypeStruct((tok, width...  6.06 us

profile of v2, /device:TPU:25, one launch (start us, length us, event | category | flops | bytes accessed | tf_op | source)
XLA Modules:
  0.0 51.2 jit_solution(9530964954610370713)
XLA Ops:
  0.6 44.5 %shard_map.86 = (f32[256,8192]{1,0:T(8,128)}, f32[256,128]{1,0:T(8,128)}, bf16[4,128,128]{2,1,0:T(8,128)(2,1)}) custom-call(bf16[256,8192]{1,0:T(8,128)(2,1)} %q_hbm.1, bf16[256,8192]{1,0:T(8,128)(2,1)} %k_hbm.1, bf16[256,8192]{1,0:T(8,128)(2,1)} %v_hbm.1, bf16[256,8192]{1,0:T(8,128)(2,1)} %g_hbm.1, bf16[64,256]{1,0:T(8,128)(2,1)} %bitcast.2, ...), custom_call_target="tpu_custom_call" | custom-call | tf_op jit(solution)/shard_map/pallas_call | solution.py:404
  45.1 6.1 %shard_map.87 = (bf16[256,8192]{1,0:T(8,128)(2,1)}, f32[4,128,128]{2,1,0:T(8,128)}) custom-call(f32[256,8192]{1,0:T(8,128)} %get-tuple-element.5.mix_ref, f32[256,128]{1,0:T(8,128)} %get-tuple-element.6.inv_ref, bf16[4,128,128]{2,1,0:T(8,128)(2,1)} %get-tuple-element.7.fin_in), custom_call_target="tpu_custom_call" | custom-call | tf_op jit(solution)/shard_map/pallas_call | solution.py:419

commit v3 on v2

--- a/solution.py
+++ b/solution.py
@@ -18,7 +18,7 @@
 HOP_LAG = 2
 E_LAG = 4
 X_LAG = 2
-FINISH_PARTS = 4
+FINISH_PARTS = 2
 F32, BF16 = jnp.float32, jnp.bfloat16
 MESH = pl.DeviceIdType.MESH
 
@@ -87,11 +87,11 @@
     lax.fori_loop(0, chunks, start_qg, 0)
 
     n_docs = docs_ref.shape[0]
-    rows = lax.broadcasted_iota(jnp.int32, (tok, tok), 0)
-    lanes = lax.broadcasted_iota(jnp.int32, (tok, tok), 1)
+    rows = lax.broadcasted_iota(jnp.int32, (tok, D), 0)
+    lanes = lax.broadcasted_iota(jnp.int32, (1, tok), 1)
     base = me * tok
-    doc_col = jnp.zeros((tok, tok), jnp.int32)
-    doc_row = jnp.zeros((tok, tok), jnp.int32)
+    doc_col = jnp.zeros((tok, D), jnp.int32)
+    doc_row = jnp.zeros((1, tok), jnp.int32)
     before = jnp.int32(0)
     last = jnp.int32(0)
     end = jnp.int32(0)
@@ -101,8 +101,8 @@
         doc_row = doc_row + jnp.where(lanes + base >= end, 1, 0)
         before = before + jnp.where(base - 1 >= end, 1, 0)
         last = last + jnp.where(base + tok - 1 >= end, 1, 0)
-    causal = rows >= lanes
-    pen_s[...] = jnp.where(causal & (doc_col == doc_row), 0.0, -1e30).astype(F32)
+    causal = lax.broadcasted_iota(jnp.int32, (tok, tok), 0) >= lax.broadcasted_iota(jnp.int32, (tok, tok), 1)
+    pen_s[...] = jnp.where(causal & (doc_col[:, :1] == doc_row), 0.0, -1e30).astype(F32)
     tri = jnp.where(causal, 1.0, 0.0).astype(BF16)
     ld = ld_ref[...]
     cum = dot(tri, ld, ((1,), (1,)))
@@ -264,7 +264,7 @@
         x_copy(j).start()
 
     def store(j):
-        return pltpu.make_async_copy(mix_s.at[:, cols(j)], mix_hbm.at[:, cols(j)], out_sem.at[j])
+        return pltpu.make_async_copy(g_s.at[:, cols(j)], mix_hbm.at[:, cols(j)], out_sem.at[j])
 
     def across(j):
         x_copy(j).wait_recv()
@@ -276,7 +276,7 @@
             mixed = mix_s[:, hcol(j, t)] + lj[:, t:t + 1] * dot(q_s[:, hcol(j, t)], st, ((1,), (0,)))
             acc = acc + mixed * mixed
             gate = g_s[:, hcol(j, t)].astype(F32)
-            mix_s[:, hcol(j, t)] = mixed * (gain_ref[:, hcol(j, t)] * jax.nn.sigmoid(gate))
+            g_s[:, hcol(j, t)] = (mixed * (gain_ref[:, hcol(j, t)] * (0.5 * jnp.tanh(0.5 * gate) + 0.5))).astype(BF16)
         ssq_s[...] = acc
         store(j).start()
 
@@ -368,7 +368,7 @@
     inv = inv_ref[...]
     for t in range(mix_ref.shape[1] // D):
         at = slice(t * D, (t + 1) * D)
-        out_ref[:, at] = (mix_ref[:, at] * inv).astype(BF16)
+        out_ref[:, at] = (mix_ref[:, at].astype(F32) * inv).astype(BF16)
     fin_ref[...] = fin_in[...].astype(F32)
 
 
@@ -404,7 +404,7 @@
     mixed, squares, final = pl.pallas_call(
         functools.partial(kernel, n, heads, chunks),
         out_shape=(
-            jax.ShapeDtypeStruct((tok, width), F32),
+            jax.ShapeDtypeStruct((tok, width), BF16),
             jax.ShapeDtypeStruct((tok, D), F32),
             jax.ShapeDtypeStruct((hn, D, D), BF16),
         ),

time: 51.5 us -> 49.5 us (0.961)
  Pallas kernels: 50.5 us -> 48.6 us
    pallas_call x1, Pallas kernels: 6.06 us -> 4.21 us  [shards(): pl.pallas_call(finish_kernel, out_shape=(jax.ShapeDtypeStruct((tok, width...]
where the time goes in v3:
time: 49.5 us; the launch traced here: 49.2 us
  Pallas kernels  48.6 us (98%)
  between operations  0.64 us (1%)
    pallas_call x1, Pallas kernels, shards(): pl.pallas_call(functools.partial(kernel, n, heads, chunks), out_shape=(ja...  44.3 us
    pallas_call x1, Pallas kernels, shards(): pl.pallas_call(finish_kernel, out_shape=(jax.ShapeDtypeStruct((tok, width...  4.21 us

profile of v3, /device:TPU:25, one launch (start us, length us, event | category | flops | bytes accessed | tf_op | source)
XLA Modules:
  0.0 49.2 jit_solution(567439996977301341)
XLA Ops:
  0.6 44.3 %shard_map.86 = (bf16[256,8192]{1,0:T(8,128)(2,1)}, f32[256,128]{1,0:T(8,128)}, bf16[4,128,128]{2,1,0:T(8,128)(2,1)}) custom-call(bf16[256,8192]{1,0:T(8,128)(2,1)} %q_hbm.1, bf16[256,8192]{1,0:T(8,128)(2,1)} %k_hbm.1, bf16[256,8192]{1,0:T(8,128)(2,1)} %v_hbm.1, bf16[256,8192]{1,0:T(8,128)(2,1)} %g_hbm.1, bf16[64,256]{1,0:T(8,128)(2,1)} %bitcast.2, ...), custom_call_target="tpu_custom_call" | custom-call | tf_op jit(solution)/shard_map/pallas_call | solution.py:404
  45.0 4.2 %shard_map.87 = (bf16[256,8192]{1,0:T(8,128)(2,1)}, f32[4,128,128]{2,1,0:T(8,128)}) custom-call(bf16[256,8192]{1,0:T(8,128)(2,1)} %get-tuple-element.5.mix_ref, f32[256,128]{1,0:T(8,128)} %get-tuple-element.6.inv_ref, bf16[4,128,128]{2,1,0:T(8,128)(2,1)} %get-tuple-element.7.fin_in), custom_call_target="tpu_custom_call" | custom-call | tf_op jit(solution)/shard_map/pallas_call | solution.py:419
